TPU v7x, 32 devices: a whole 2x2x4 slice. The times are simulated.
32 devices in a mesh: rep: 4 (over y, x), ep: 8 (over z, core).
Axes of the slice: x: 2, y: 2, z: 4, core: 2. Of those that a mesh axis runs over, the one named last changes fastest.
Arguments:
- tokens: bfloat16 [2, 8, 4, 4, 4096], P(None, 'ep', 'rep'), may hold values from -6 to 6
- norm_gain: float32 [4096], replicated, may hold values from 0.5 to 1.5
- expert_ids: int32 [2, 8, 4, 4, 8], P(None, 'ep'), may hold values from 0 to 15, all different within a row; in each aligned block of 16 rows (0 to 15, 16 to 31, ..., all dimensions but the last counted through in order) at most 10 rows name the same one
- route_weights: float32 [2, 8, 4, 4, 8], P(None, 'ep'), may hold values from 0.05 to 1
- w_gate: bfloat16 [16, 1536, 4096], P('ep', 'rep'), may hold values from -0.09375 to 0.09375
- w_up: bfloat16 [16, 1536, 4096], P('ep', 'rep'), may hold values from -0.09375 to 0.09375
- w_down: bfloat16 [16, 1536, 4096], P('ep', 'rep'), may hold values from -0.15625 to 0.15625
Outputs:
- mixed: bfloat16 [2, 8, 4, 4, 4096], P(None, 'ep', 'rep')
Inputs may be any that keep to these rules, and one draw needn't show every extreme that they name: `expert_ids`: each row names 8 different experts. In each step, among the rows of one index of ep (16 rows, an aligned block), no expert is named by more than 10 rows, a bound that some block reaches.
All inputs are finite; a program needn't handle non-finite values.
Results may differ from a plain program's by a relative error of at most 0.014.
Values may be sent and summed in bfloat16 or wider, within the bound.
A program may use at most 128 MiB of HBM per device.

v0:
```python
import jax
import jax.numpy as jnp
from jax import lax
from jax.sharding import PartitionSpec as P

epsilon = 1e-06


def norm_rows(values, gain_values):
    widened = values.astype(jnp.float32)
    scaled = lax.rsqrt(jnp.mean(widened * widened, axis=-1, keepdims=True) + epsilon)
    return (widened * scaled * gain_values).astype(jnp.bfloat16)


def expert_partial(slot_rows, gate_weight, up_weight, down_weight):
    contract_last = (((1,), (1,)), ((), ()))
    gate_out = lax.dot_general(
        slot_rows, gate_weight, contract_last, preferred_element_type=jnp.float32
    )
    up_out = lax.dot_general(
        slot_rows, up_weight, contract_last, preferred_element_type=jnp.float32
    )
    hidden = (jax.nn.silu(gate_out) * up_out).astype(jnp.bfloat16)
    return jnp.dot(hidden, down_weight, preferred_element_type=jnp.float32).astype(jnp.bfloat16)


def weigh_choices(shares, picked):
    choice_total = picked.shape[1]
    weighted = shares[:, 0:1] * picked[:, 0]
    for which in range(1, choice_total):
        weighted = weighted + shares[:, which : which + 1] * picked[:, which]
    return weighted


def on_device(tokens, norm_gain, expert_ids, route_weights, w_gate, w_up, w_down):
    ep_size = lax.axis_size("ep")
    rep_size = lax.axis_size("rep")
    step_count = tokens.shape[0]
    row_count = tokens.shape[3]
    model_width = tokens.shape[4]
    choice_count = expert_ids.shape[4]
    local_experts = w_gate.shape[0]
    experts = local_experts * ep_size
    block_rows = rep_size * row_count
    capacity = block_rows * choice_count * 5 // (4 * experts)
    column_width = model_width // rep_size
    assigned = block_rows * choice_count
    row_of = jnp.arange(assigned, dtype=jnp.int32) // choice_count
    outputs = []
    for step_index in range(step_count):
        own_normed = norm_rows(tokens[step_index, 0, 0], norm_gain)
        step_weights = route_weights[step_index].reshape(block_rows, choice_count)
        shares = step_weights / jnp.sum(step_weights, axis=1, keepdims=True)
        chosen_ids = expert_ids[step_index].reshape(assigned)
        target = chosen_ids // local_experts
        slot_index = chosen_ids % local_experts
        buckets = ep_size * local_experts
        bucket = target * local_experts + slot_index
        onehot = (bucket[:, None] == jnp.arange(buckets, dtype=jnp.int32)[None, :]).astype(
            jnp.int32
        )
        position = jnp.sum((jnp.cumsum(onehot, axis=0) - onehot) * onehot, axis=1)
        flat_index = bucket * capacity + position
        source_row = (
            jnp.full((buckets * capacity,), block_rows, jnp.int32).at[flat_index].set(row_of)
        )
        own_part = lax.all_to_all(own_normed, "rep", split_axis=1, concat_axis=0, tiled=True)
        padded = jnp.concatenate([own_part, jnp.zeros((1, column_width), jnp.bfloat16)], axis=0)
        outgoing = jnp.take(padded, source_row, axis=0).reshape(
            ep_size, local_experts, capacity, column_width
        )
        received = lax.all_to_all(outgoing, "ep", split_axis=0, concat_axis=0, tiled=True)
        arrived = lax.all_gather(received, "rep", axis=3, tiled=True)
        slot_results = []
        for local_slot in range(local_experts):
            weights_now = (w_gate[local_slot], w_up[local_slot], w_down[local_slot])
            slot_rows = arrived[:, local_slot].reshape(ep_size * capacity, model_width)
            slot_out = expert_partial(slot_rows, weights_now[0], weights_now[1], weights_now[2])
            slot_results.append(slot_out.reshape(ep_size, capacity, model_width))
        results_out = jnp.stack(slot_results, axis=1)
        summed = lax.psum_scatter(
            results_out.astype(jnp.float32).astype(jnp.bfloat16),
            "rep",
            scatter_dimension=3,
            tiled=True,
        ).astype(jnp.float32)
        back = lax.all_to_all(
            summed.astype(jnp.bfloat16), "ep", split_axis=0, concat_axis=0, tiled=True
        ).astype(summed.dtype)
        picked = jnp.take(back.reshape(buckets * capacity, column_width), flat_index, axis=0)
        picked = picked.reshape(block_rows, choice_count, column_width)
        weighted = weigh_choices(shares, picked)
        mixed = (
            lax.all_to_all(
                weighted.astype(jnp.bfloat16), "rep", split_axis=0, concat_axis=1, tiled=True
            )
            .astype(weighted.dtype)
            .astype(jnp.bfloat16)
        )
        outputs.append(mixed)
    return jnp.stack(outputs)[:, None, None]


def solution(mesh):
    return jax.shard_map(
        on_device,
        mesh=mesh,
        in_specs=(
            P(None, "ep", "rep", None, None),
            P(),
            P(None, "ep", None, None, None),
            P(None, "ep", None, None, None),
            P("ep", "rep", None),
            P("ep", "rep", None),
            P("ep", "rep", None),
        ),
        out_specs=P(None, "ep", "rep", None, None),
        check_vma=False,
    )
```

profile of v0, /device:TPU:0, one launch (start us, length us, event | category | flops | bytes accessed | tf_op | source)
XLA Modules:
  0.0 218.7 jit_solution(7675640951813807091)
XLA Ops:
  6.5 0.9 multiply_reduce_fusion.1
  7.5 0.8 slice_convert_fusion.1
  8.3 0.7 mul.310
  9.0 0.7 multiply_convert_fusion.1
  9.7 5.2 %all-to-all-start = ((bf16[4,4,1024]{2,0,1:T(4,128)(2,1)}), bf16[4,4,1024]{2,0,1:T(4,128)(2,1)S(1)}, u32[]{:S(2)}, u32[]{:S(2)}) async-start(bf16[4,4,1024]{2,0,1:T(4,128)(2,1)} %get-tuple-element.56), calls=%async_computation | async-start | bytes 65536 | tf_op jit(solution)/shard_map/all_to_all | solution.py:67
  14.9 0.7 fusion.104
  16.3 1.0 scatter_custom_fusion
  17.4 2.3 %all-to-all-done = bf16[4,4,1024]{2,0,1:T(4,128)(2,1)S(1)} async-done(((bf16[4,4,1024]{2,0,1:T(4,128)(2,1)}), bf16[4,4,1024]{2,0,1:T(4,128)(2,1)S(1)}, u32[]{:S(2)}, u32[]{:S(2)}) %all-to-all-start) | async-done | bytes 32800 | tf_op jit(solution)/shard_map/all_to_all | solution.py:67
  19.7 0.9 gather_fusion
  20.9 1.0 copy.89
  21.9 4.9 %all-to-all-start.1 = ((bf16[8,2,10,1024]{3,1,2,0:T(2,128)(2,1)}), bf16[8,2,10,1024]{3,1,2,0:T(2,128)(2,1)S(1)}, u32[]{:S(2)}, u32[]{:S(2)}) async-start(bf16[8,2,10,1024]{3,1,2,0:T(2,128)(2,1)} %copy.89), calls=%async_computation.1 | async-start | bytes 655360 | tf_op jit(solution)/shard_map/all_to_all | solution.py:72
  26.9 11.0 %all-to-all-done.1 = bf16[8,2,10,1024]{3,1,2,0:T(2,128)(2,1)S(1)} async-done(((bf16[8,2,10,1024]{3,1,2,0:T(2,128)(2,1)}), bf16[8,2,10,1024]{3,1,2,0:T(2,128)(2,1)S(1)}, u32[]{:S(2)}, u32[]{:S(2)}) %all-to-all-start.1) | async-done | bytes 327712 | tf_op jit(solution)/shard_map/all_to_all | solution.py:72
  37.9 3.3 %all-to-all-start.4 = ((bf16[4,4,1024]{2,0,1:T(4,128)(2,1)}), bf16[4,4,1024]{2,0,1:T(4,128)(2,1)S(1)}, u32[]{:S(2)}, u32[]{:S(2)}) async-start(bf16[4,4,1024]{2,0,1:T(4,128)(2,1)} %get-tuple-element.57), calls=%async_computation.5 | async-start | bytes 65536 | tf_op jit(solution)/shard_map/all_to_all | solution.py:67
  41.3 0.7 all-gather.3.cloned.1.call-update
  42.6 1.0 scatter_custom_fusion.1
  43.6 2.3 %all-to-all-done.4 = bf16[4,4,1024]{2,0,1:T(4,128)(2,1)S(1)} async-done(((bf16[4,4,1024]{2,0,1:T(4,128)(2,1)}), bf16[4,4,1024]{2,0,1:T(4,128)(2,1)S(1)}, u32[]{:S(2)}, u32[]{:S(2)}) %all-to-all-start.4) | async-done | bytes 32800 | tf_op jit(solution)/shard_map/all_to_all | solution.py:67
  46.0 0.9 gather_fusion.2
  47.5 14.2 %all_to_all.78 = bf16[8,2,10,1024]{3,1,2,0:T(2,128)(2,1)} all-to-all(bf16[8,2,10,1024]{3,1,2,0:T(2,128)(2,1)S(1)} %copy.94), channel_id=1, replica_groups=mesh['rep'=4,'ep'=8] {'ep'}, dimensions={0} | all-to-all | bytes 655360 | tf_op jit(solution)/shard_map/all_to_all | solution.py:72
  61.9 9.9 %all-gather.3.cloned.1.call-done = bf16[8,2,10,4096]{3,1,2,0:T(2,128)(2,1)} async-done(((bf16[8,2,10,1024]{3,1,2,0:T(2,128)(2,1)}), bf16[8,2,10,4096]{3,1,2,0:T(2,128)(2,1)}) %all-gather.3.cloned.1.call-update) | async-done | bytes 1310736 | tf_op jit(solution)/shard_map/all_gather | solution.py:73
  71.8 7.6 %slice_reduce_fusion.3 = (bf16[8,10,4096]{2,1,0:T(8,128)(2,1)S(1)}, bf16[8,10,4096]{2,1,0:T(8,128)(2,1)S(1)}) fusion(bf16[8,2,10,4096]{3,1,2,0:T(2,128)(2,1)} %all-gather.3.cloned.1.call-done), kind=kLoop, calls=%fused_computation.47 | loop fusion | bytes 2621440 | tf_op jit(solution)/shard_map/slice | solution.py:77
  79.6 3.1 %fusion.18 = f32[80,384]{1,0:T(8,128)S(1)} fusion(bf16[80,4096]{1,0:T(8,128)(2,1)S(1)} %reshape_squeeze.31, bf16[2,384,4096]{2,1,0:T(8,128)(2,1)} %param.15), kind=kOutput, calls=%fused_computation.28 | convolution fusion | flops 251658240 | bytes 3923968 | tf_op jit(solution)/shard_map/dot_general | solution.py:17
  82.7 5.0 %convolution_convert_fusion.3 = bf16[80,4096]{1,0:T(8,128)(2,1)S(1)} fusion(bf16[2,384,4096]{2,1,0:T(8,128)(2,1)} %param.17, bf16[80,4096]{1,0:T(8,128)(2,1)S(1)} %reshape_squeeze.31, bf16[2,384,4096]{2,1,0:T(8,128)(2,1)} %param.16, f32[80,384]{1,0:T(8,128)S(1)} %fusion.18), kind=kOutput, calls=%fused_computation.9 | convolution fusion | flops 503828480 | bytes 7725056 | tf_op jit(solution)/shard_map/dot_general | solution.py:24
  88.2 3.0 %fusion.8 = f32[80,384]{1,0:T(8,128)S(1)} fusion(bf16[80,4096]{1,0:T(8,128)(2,1)S(1)} %reshape_squeeze.32, bf16[2,384,4096]{2,1,0:T(8,128)(2,1)} %param.15), kind=kOutput, calls=%fused_computation.18 | convolution fusion | flops 251658240 | bytes 3923968 | tf_op jit(solution)/shard_map/dot_general | solution.py:17
  91.1 5.1 %convolution_convert_fusion.2 = bf16[80,4096]{1,0:T(8,128)(2,1)S(1)} fusion(bf16[2,384,4096]{2,1,0:T(8,128)(2,1)} %param.17, bf16[80,4096]{1,0:T(8,128)(2,1)S(1)} %reshape_squeeze.32, bf16[2,384,4096]{2,1,0:T(8,128)(2,1)} %param.16, f32[80,384]{1,0:T(8,128)S(1)} %fusion.8), kind=kOutput, calls=%fused_computation.8 | convolution fusion | flops 503828480 | bytes 7725056 | tf_op jit(solution)/shard_map/dot_general | solution.py:24
  96.5 1.6 pad_maximum_fusion
  98.4 3.8 %all-gather.5.cloned.1.call-done = bf16[8,2,10,4096]{3,1,2,0:T(2,128)(2,1)} async-done(((bf16[8,2,10,1024]{3,1,2,0:T(2,128)(2,1)}), bf16[8,2,10,4096]{3,1,2,0:T(2,128)(2,1)}) %all-gather.5.cloned.1.call-update) | async-done | bytes 1310736 | tf_op jit(solution)/shard_map/all_gather | solution.py:73
  102.2 7.6 %slice_reduce_fusion.1 = (bf16[8,10,4096]{2,1,0:T(8,128)(2,1)S(1)}, bf16[8,10,4096]{2,1,0:T(8,128)(2,1)S(1)}) fusion(bf16[8,2,10,4096]{3,1,2,0:T(2,128)(2,1)} %all-gather.5.cloned.1.call-done), kind=kLoop, calls=%fused_computation.45 | loop fusion | bytes 2621440 | tf_op jit(solution)/shard_map/slice | solution.py:77
  110.0 3.1 %fusion.16 = f32[80,384]{1,0:T(8,128)S(1)} fusion(bf16[80,4096]{1,0:T(8,128)(2,1)S(1)} %reshape_squeeze.36, bf16[2,384,4096]{2,1,0:T(8,128)(2,1)} %param.15), kind=kOutput, calls=%fused_computation.26 | convolution fusion | flops 251658240 | bytes 3923968 | tf_op jit(solution)/shard_map/dot_general | solution.py:17
  113.1 5.0 %convolution_convert_fusion.1 = bf16[80,4096]{1,0:T(8,128)(2,1)S(1)} fusion(bf16[2,384,4096]{2,1,0:T(8,128)(2,1)} %param.17, bf16[80,4096]{1,0:T(8,128)(2,1)S(1)} %reshape_squeeze.36, bf16[2,384,4096]{2,1,0:T(8,128)(2,1)} %param.16, f32[80,384]{1,0:T(8,128)S(1)} %fusion.16), kind=kOutput, calls=%fused_computation.7 | convolution fusion | flops 503828480 | bytes 7725056 | tf_op jit(solution)/shard_map/dot_general | solution.py:24
  118.5 3.1 %fusion.6 = f32[80,384]{1,0:T(8,128)S(1)} fusion(bf16[80,4096]{1,0:T(8,128)(2,1)S(1)} %reshape_squeeze.37, bf16[2,384,4096]{2,1,0:T(8,128)(2,1)} %param.15), kind=kOutput, calls=%fused_computation.16 | convolution fusion | flops 251658240 | bytes 3923968 | tf_op jit(solution)/shard_map/dot_general | solution.py:17
  121.7 5.1 %convolution_convert_fusion = bf16[80,4096]{1,0:T(8,128)(2,1)S(1)} fusion(bf16[2,384,4096]{2,1,0:T(8,128)(2,1)} %param.17, bf16[80,4096]{1,0:T(8,128)(2,1)S(1)} %reshape_squeeze.37, bf16[2,384,4096]{2,1,0:T(8,128)(2,1)} %param.16, f32[80,384]{1,0:T(8,128)S(1)} %fusion.6), kind=kOutput, calls=%fused_computation.6 | convolution fusion | flops 503828480 | bytes 7725056 | tf_op jit(solution)/shard_map/dot_general | solution.py:24
  127.0 1.6 pad_maximum_fusion.1
  131.2 9.2 %reduce-scatter.3.cloned.1.call-done = bf16[8,2,10,1024]{3,2,0,1:T(8,128)(2,1)} async-done(((bf16[8,2,10,4096]{3,2,0,1:T(8,128)(2,1)}), bf16[8,2,10,1024]{3,2,0,1:T(8,128)(2,1)}) %reduce-scatter.3.cloned.1.call-update) | async-done | bytes 327696 | tf_op jit(solution)/shard_map/reduce_scatter | solution.py:81
  140.4 2.1 copy.90
  142.4 4.6 %all-to-all-start.2 = ((bf16[8,2,10,1024]{3,1,2,0:T(2,128)(2,1)}), bf16[8,2,10,1024]{3,1,2,0:T(2,128)(2,1)S(1)}, u32[]{:S(2)}, u32[]{:S(2)}) async-start(bf16[8,2,10,1024]{3,1,2,0:T(2,128)(2,1)} %copy.90), calls=%async_computation.3 | async-start | bytes 655360 | tf_op jit(solution)/shard_map/all_to_all | solution.py:87
  147.1 31.3 %reduce-scatter.5.cloned.1.call-done = bf16[8,2,10,1024]{3,2,0,1:T(8,128)(2,1)} async-done(((bf16[8,2,10,4096]{3,2,0,1:T(8,128)(2,1)}), bf16[8,2,10,1024]{3,2,0,1:T(8,128)(2,1)}) %reduce-scatter.5.cloned.1.call-update) | async-done | bytes 327696 | tf_op jit(solution)/shard_map/reduce_scatter | solution.py:81
  178.4 2.1 copy.95
  180.5 4.6 %all-to-all-start.6 = ((bf16[8,2,10,1024]{3,1,2,0:T(2,128)(2,1)}), bf16[8,2,10,1024]{3,1,2,0:T(2,128)(2,1)S(1)}, u32[]{:S(2)}, u32[]{:S(2)}) async-start(bf16[8,2,10,1024]{3,1,2,0:T(2,128)(2,1)} %copy.95), calls=%async_computation.8 | async-start | bytes 655360 | tf_op jit(solution)/shard_map/all_to_all | solution.py:87
  185.7 0.8 gather_fusion.1
  186.6 1.3 slice_reduce_fusion.19
  188.2 0.8 add_convert_fusion.1
  189.0 7.2 %all-to-all-done.6 = bf16[8,2,10,1024]{3,1,2,0:T(2,128)(2,1)S(1)} async-done(((bf16[8,2,10,1024]{3,1,2,0:T(2,128)(2,1)}), bf16[8,2,10,1024]{3,1,2,0:T(2,128)(2,1)S(1)}, u32[]{:S(2)}, u32[]{:S(2)}) %all-to-all-start.6) | async-done | bytes 327712 | tf_op jit(solution)/shard_map/all_to_all | solution.py:87
  196.2 3.3 %all-to-all-start.3 = ((bf16[4,4,1024]{2,1,0:T(4,128)(2,1)}), bf16[4,4,1024]{2,1,0:T(4,128)(2,1)S(1)}, u32[]{:S(2)}, u32[]{:S(2)}) async-start(bf16[4,4,1024]{2,1,0:T(4,128)(2,1)} %add_convert_fusion.1), calls=%async_computation.4 | async-start | bytes 65536 | tf_op jit(solution)/shard_map/all_to_all | solution.py:94
  200.1 0.8 gather_fusion.3
  201.0 1.3 slice_reduce_fusion.11
  202.8 1.4 all-to-all-done.3
  204.2 7.3 %all_to_all.79 = bf16[4,4,1024]{2,1,0:T(4,128)(2,1)S(1)} all-to-all(bf16[4,4,1024]{2,1,0:T(4,128)(2,1)S(1)} %add_convert_fusion), channel_id=1, replica_groups=mesh['rep'=4,'ep'=8] {'rep'}, dimensions={0} | all-to-all | bytes 65536 | tf_op jit(solution)/shard_map/all_to_all | solution.py:94
  211.5 0.7 maximum_bitcast_fusion
  (103 shorter events, 9.1 us)
Async XLA Ops:
  9.7 9.9 %all-to-all-start = ((bf16[4,4,1024]{2,0,1:T(4,128)(2,1)}), bf16[4,4,1024]{2,0,1:T(4,128)(2,1)S(1)}, u32[]{:S(2)}, u32[]{:S(2)}) async-start(bf16[4,4,1024]{2,0,1:T(4,128)(2,1)} %get-tuple-element.56), calls=%async_computation | async-start | bytes 65536 | tf_op jit(solution)/shard_map/all_to_all | solution.py:67
  21.9 16.0 %all-to-all-start.1 = ((bf16[8,2,10,1024]{3,1,2,0:T(2,128)(2,1)}), bf16[8,2,10,1024]{3,1,2,0:T(2,128)(2,1)S(1)}, u32[]{:S(2)}, u32[]{:S(2)}) async-start(bf16[8,2,10,1024]{3,1,2,0:T(2,128)(2,1)} %copy.89), calls=%async_computation.1 | async-start | bytes 655360 | tf_op jit(solution)/shard_map/all_to_all | solution.py:72
  37.9 3.3 %copy-start = (bf16[8,2,10,1024]{3,1,2,0:T(2,128)(2,1)}, bf16[8,2,10,1024]{3,1,2,0:T(2,128)(2,1)S(1)}, u32[]{:S(2)}) copy-start(bf16[8,2,10,1024]{3,1,2,0:T(2,128)(2,1)S(1)} %all-to-all-done.1) | copy-start | bytes 983044
  37.9 8.0 %all-to-all-start.4 = ((bf16[4,4,1024]{2,0,1:T(4,128)(2,1)}), bf16[4,4,1024]{2,0,1:T(4,128)(2,1)S(1)}, u32[]{:S(2)}, u32[]{:S(2)}) async-start(bf16[4,4,1024]{2,0,1:T(4,128)(2,1)} %get-tuple-element.57), calls=%async_computation.5 | async-start | bytes 65536 | tf_op jit(solution)/shard_map/all_to_all | solution.py:67
  41.2 30.6 %all-gather.3.cloned.1.call-start = ((), (), s32[]{:S(2)}) async-start(), calls=%async_computation.10 | async-start | bytes 1638400 | tf_op jit(solution)/shard_map/all_gather | solution.py:73
  41.9 60.2 %all-gather.5.cloned.1.call-start = ((), (), s32[]{:S(2)}) async-start(), calls=%async_computation.12 | async-start | bytes 1638400 | tf_op jit(solution)/shard_map/all_gather | solution.py:73
  61.7 78.7 %reduce-scatter.3.cloned.1.call-start = ((), (), s32[]{:S(2)}) async-start(), calls=%async_computation.11 | async-start | bytes 2621440 | tf_op jit(solution)/shard_map/reduce_scatter | solution.py:81
  98.1 80.2 %reduce-scatter.5.cloned.1.call-start = ((), (), s32[]{:S(2)}) async-start(), calls=%async_computation.13 | async-start | bytes 2621440 | tf_op jit(solution)/shard_map/reduce_scatter | solution.py:81
  127.0 1.6 copy-start.1
  142.4 38.1 %all-to-all-start.2 = ((bf16[8,2,10,1024]{3,1,2,0:T(2,128)(2,1)}), bf16[8,2,10,1024]{3,1,2,0:T(2,128)(2,1)S(1)}, u32[]{:S(2)}, u32[]{:S(2)}) async-start(bf16[8,2,10,1024]{3,1,2,0:T(2,128)(2,1)} %copy.90), calls=%async_computation.3 | async-start | bytes 655360 | tf_op jit(solution)/shard_map/all_to_all | solution.py:87
  180.5 15.7 %all-to-all-start.6 = ((bf16[8,2,10,1024]{3,1,2,0:T(2,128)(2,1)}), bf16[8,2,10,1024]{3,1,2,0:T(2,128)(2,1)S(1)}, u32[]{:S(2)}, u32[]{:S(2)}) async-start(bf16[8,2,10,1024]{3,1,2,0:T(2,128)(2,1)} %copy.95), calls=%async_computation.8 | async-start | bytes 655360 | tf_op jit(solution)/shard_map/all_to_all | solution.py:87
  196.2 8.0 %all-to-all-start.3 = ((bf16[4,4,1024]{2,1,0:T(4,128)(2,1)}), bf16[4,4,1024]{2,1,0:T(4,128)(2,1)S(1)}, u32[]{:S(2)}, u32[]{:S(2)}) async-start(bf16[4,4,1024]{2,1,0:T(4,128)(2,1)} %add_convert_fusion.1), calls=%async_computation.4 | async-start | bytes 65536 | tf_op jit(solution)/shard_map/all_to_all | solution.py:94
Sparse Core Ops, SparseCore 0:
  43.8 27.8 all-gather.2
  73.6 28.5 all-gather.4
  105.1 35.1 reduce-scatter.2
  143.2 35.1 reduce-scatter.4
where the time goes:
time: 220 us; the launch traced here: 219 us
  waiting for transfers between devices  79.2 us (36%)
  local copies, waits for them, and re-layouts  36.5 us (17%)
  matrix products  32.4 us (15%)
  starting transfers between devices  26.4 us (12%)
  blocking collectives  21.5 us (10%)
  between operations  13.7 us (6%)
  other arithmetic  9.1 us (4%)
    reduce_scatter x2, waiting for transfers between devices, on_device(): lax.psum_scatter(results_out.astype(jnp.float32).astype(jnp.bfloat16), 'r...  40.5 us
    dot_general x4, matrix products, expert_partial(): jnp.dot(hidden, down_weight, preferred_element_type=jnp.float32)  20.1 us
    slice x2, local copies, waits for them, and re-layouts, on_device(): slot_rows = arrived[:, local_slot].reshape(ep_size * capacity, model_width)  15.2 us
    all_to_all x1, blocking collectives, on_device(): lax.all_to_all(outgoing, 'ep', split_axis=0, concat_axis=0, tiled=True)  14.2 us
    all_gather x2, waiting for transfers between devices, on_device(): arrived = lax.all_gather(received, 'rep', axis=3, tiled=True)  13.6 us
    dot_general x4, matrix products, expert_partial(): lax.dot_general(slot_rows, gate_weight, contract_last, preferred_element_...  12.3 us
    all_to_all x1, waiting for transfers between devices, on_device(): lax.all_to_all(outgoing, 'ep', split_axis=0, concat_axis=0, tiled=True)  11 us
    all_to_all x2, starting transfers between devices, on_device(): lax.all_to_all(summed.astype(jnp.bfloat16), 'ep', split_axis=0, concat_ax...  9.22 us
  transfers between devices with their start and end apart: 10, of which 9 were waited for; matrix products, arithmetic and copies ran while one was open for 33% of the time, Pallas kernels for 0%

commit v1 on v0

--- a/solution.py
+++ b/solution.py
@@ -1,6 +1,8 @@
 import jax
 import jax.numpy as jnp
 from jax import lax
+from jax.experimental import pallas as pl
+from jax.experimental.pallas import tpu as pltpu
 from jax.sharding import PartitionSpec as P
 
 epsilon = 1e-06
@@ -32,7 +34,7 @@
     return weighted
 
 
-def on_device(tokens, norm_gain, expert_ids, route_weights, w_gate, w_up, w_down):
+def routed_on_device(tokens, norm_gain, expert_ids, route_weights, w_gate, w_up, w_down):
     ep_size = lax.axis_size("ep")
     rep_size = lax.axis_size("rep")
     step_count = tokens.shape[0]
@@ -101,6 +103,304 @@
     return jnp.stack(outputs)[:, None, None]
 
 
+LANES = 128
+HALF = LANES // 2
+CHUNKS = 4
+
+
+def fused_kernel(
+    tok_ref, gain_ref, ids_ref, rw_ref, gate_hbm, up_hbm, down_hbm, out_ref,
+    wgu, wdn, xg, wx, xs, acc, hs, nrm, wst,
+    pbuf, rb0, sb1, rb1, sb2, rb2, sb3, sv, rb3, ost,
+    wsem, ag_send, ag_recv, rs_send, rs_recv,
+):
+    f32, bf16 = jnp.float32, jnp.bfloat16
+    steps, rows, width = tok_ref.shape
+    nz = xg.shape[4]
+    cw = xg.shape[6]
+    own_rows = steps * rows
+    local_experts, hidden_units = gate_hbm.shape[0], gate_hbm.shape[1]
+    choices = ids_ref.shape[3]
+    total = 8 * nz * own_rows
+    rep, ep = lax.axis_index("rep"), lax.axis_index("ep")
+    y, x = rep // 2, rep % 2
+    z, core = ep // 2, ep % 2
+    partner = (rep, z * 2 + 1 - core)
+    over_x = (y * 2 + 1 - x, ep)
+    over_y = ((1 - y) * 2 + x, ep)
+    along_z = [(rep, ((z + d) % nz) * 2 + core) for d in range(1, nz)]
+
+    barrier = pltpu.get_barrier_semaphore()
+    everyone = [partner, over_x, over_y] + along_z
+    for device in everyone:
+        pl.semaphore_signal(barrier, inc=1, device_id=device, device_id_type=pl.DeviceIdType.MESH)
+
+    loads = []
+    for j in range(local_experts):
+        loads.append(pltpu.make_async_copy(gate_hbm.at[j], wgu.at[j], wsem.at[len(loads)]))
+        loads.append(pltpu.make_async_copy(up_hbm.at[j], wgu.at[local_experts + j], wsem.at[len(loads)]))
+    downs = []
+    for j in range(local_experts):
+        downs.append(
+            pltpu.make_async_copy(
+                down_hbm.at[j],
+                wdn.at[pl.ds(j * hidden_units, hidden_units)],
+                wsem.at[len(loads) + j],
+            )
+        )
+    for load in loads + downs:
+        load.start()
+
+    lane = lax.broadcasted_iota(jnp.int32, (rows, LANES), 1)
+    for s in range(steps):
+        nrm[pl.ds(s * rows, rows), :] = tok_ref[s].astype(f32)
+        weights_now = rw_ref[s, rep]
+        ids_now = ids_ref[s, rep]
+        shares = weights_now / jnp.sum(weights_now, axis=1, keepdims=True)
+        dense = jnp.zeros((rows, LANES), f32)
+        for k in range(choices):
+            dense = dense + jnp.where((lane & (HALF - 1)) == ids_now[:, k : k + 1], shares[:, k : k + 1], 0.0)
+        wst[pl.ds(s * rows, rows), :] = dense
+    dense = wst[...]
+    high = dense.astype(bf16).astype(f32)
+    wide_lane = lax.broadcasted_iota(jnp.int32, (own_rows, LANES), 1)
+    wx[core, y, x, z] = jnp.where(wide_lane < HALF, high, dense - high).astype(bf16)
+    values = nrm[...]
+    scaled = lax.rsqrt(jnp.mean(values * values, axis=-1, keepdims=True) + epsilon)
+    for c in range(CHUNKS):
+        cols = pl.ds(c * cw, cw)
+        xg[c, core, y, x, z] = (nrm[:, cols] * scaled * gain_ref[:, cols]).astype(bf16)
+    pl.semaphore_wait(barrier, len(everyone))
+
+    started = []
+
+    def send(src, dst, send_sem, recv_sem, device):
+        copy = pltpu.make_async_remote_copy(
+            src_ref=src, dst_ref=dst, send_sem=send_sem, recv_sem=recv_sem,
+            device_id=device, device_id_type=pl.DeviceIdType.MESH,
+        )
+        copy.start()
+        started.append(copy)
+        return copy
+
+    bufs = [xg.at[c] for c in range(CHUNKS)] + [wx]
+    order = [CHUNKS] + list(range(CHUNKS))
+    x_first = [c % 2 == 0 for c in range(CHUNKS)] + [False]
+    first_device = [over_x if flag else over_y for flag in x_first]
+    second_device = [over_y if flag else over_x for flag in x_first]
+
+    hop_z, hop_1, hop_2, share_1, share_2, share_3 = {}, {}, {}, {}, {}, {}
+
+    def ag_send_to(c, slot, where, device):
+        ref = bufs[c].at[where]
+        return send(ref, ref, ag_send.at[c, slot], ag_recv.at[c, slot], device)
+
+    for c in order:
+        hop_z[c] = [ag_send_to(c, d, (core, y, x, z), along_z[d]) for d in range(nz - 1)]
+    for c in order:
+        for copy in hop_z[c]:
+            copy.wait_recv()
+        hop_1[c] = ag_send_to(c, nz - 1, (core, y, x), first_device[c])
+        share_1[c] = ag_send_to(c, nz + 1, (core, y, x), partner)
+    for c in order:
+        hop_1[c].wait_recv()
+        if x_first[c]:
+            hop_2[c] = ag_send_to(c, nz, (core, y), second_device[c])
+            share_2[c] = ag_send_to(c, nz + 2, (core, y, 1 - x), partner)
+        else:
+            hop_2[c] = ag_send_to(c, nz, (core, slice(None), x), second_device[c])
+            share_2[c] = ag_send_to(c, nz + 2, (core, 1 - y, x), partner)
+
+    def finish_gather(c):
+        hop_2[c].wait_recv()
+        where = (core, 1 - y) if x_first[c] else (core, slice(None), 1 - x)
+        share_3[c] = ag_send_to(c, nz + 3, where, partner)
+
+    def arrived(c):
+        for copy in (share_1[c], share_2[c], share_3[c]):
+            copy.wait_recv()
+
+    def gate_up(c):
+        arrived(c)
+        xs[...] = xg[c].astype(f32).reshape(total, cw).astype(bf16)
+        if c == 0:
+            for load in loads:
+                load.wait()
+
+        def one(i, carry):
+            part = lax.dot_general(
+                xs[...], wgu[i, :, pl.ds(c * cw, cw)],
+                (((1,), (1,)), ((), ())), preferred_element_type=f32,
+            )
+            acc[i] = part if c == 0 else acc[i] + part
+            return carry
+
+        lax.fori_loop(0, 2 * local_experts, one, 0)
+
+    for at, c in enumerate(order):
+        finish_gather(c)
+        if at >= 2:
+            gate_up(order[at - 1])
+    gate_up(order[-1])
+    arrived(CHUNKS)
+
+    row_weights = wx[...].astype(f32).reshape(total, LANES)
+    all_lane = lax.broadcasted_iota(jnp.int32, (total, LANES), 1) & (HALF - 1)
+    for j in range(local_experts):
+        mine = jnp.sum(
+            jnp.where(all_lane == ep * local_experts + j, row_weights, 0.0), axis=1, keepdims=True
+        )
+        gate_out, up_out = acc[j], acc[local_experts + j]
+        hs[:, pl.ds(j * hidden_units, hidden_units)] = (jax.nn.silu(gate_out) * up_out * mine).astype(bf16)
+    for load in downs:
+        load.wait()
+
+    to_core, to_first, to_second, to_z = {}, {}, {}, {}
+
+    def rs_send_to(c, slot, src, dst, device):
+        return send(src, dst, rs_send.at[c, slot], rs_recv.at[c, slot], device)
+
+    def place(c, first, second):
+        return (second, first) if x_first[c] else (first, second)
+
+    me_first = [x if x_first[c] else y for c in range(CHUNKS)]
+    me_second = [y if x_first[c] else x for c in range(CHUNKS)]
+
+    def pair_sum(c, first, second):
+        where = place(c, first, second)
+        return pbuf[(c, core) + where].astype(f32) + rb0[(c,) + where].astype(f32)
+
+    def down(c):
+        half = cw // 2
+        for piece in range(2):
+            part = jnp.dot(
+                hs[...], wdn[:, pl.ds(c * cw + piece * half, half)], preferred_element_type=f32
+            )
+            pbuf[c, :, :, :, :, :, pl.ds(piece * half, half)] = part.reshape(
+                2, 2, 2, nz, own_rows, half
+            ).astype(bf16)
+        to_core[c] = rs_send_to(c, nz - 1, pbuf.at[c, 1 - core], rb0.at[c], partner)
+
+    def stage_1(c):
+        to_core[c].wait_recv()
+        for second in range(2):
+            sb1[c, second] = pair_sum(c, 1 - me_first[c], second).astype(bf16)
+        to_first[c] = rs_send_to(c, nz, sb1.at[c], rb1.at[c], first_device[c])
+
+    def stage_2(c):
+        to_first[c].wait_recv()
+        other = 1 - me_second[c]
+        sb2[c] = (pair_sum(c, me_first[c], other) + rb1[c, other].astype(f32)).astype(bf16)
+        to_second[c] = rs_send_to(c, nz + 1, sb2.at[c], rb2.at[c], second_device[c])
+
+    def stage_3(c):
+        to_second[c].wait_recv()
+        mine = pair_sum(c, me_first[c], me_second[c]) + rb1[c, me_second[c]].astype(f32) + rb2[c].astype(f32)
+        sv[c] = mine
+        sb3[c] = mine.astype(bf16)
+        to_z[c] = [
+            rs_send_to(c, d, sb3.at[c, (z + d + 1) % nz], rb3.at[c, d], along_z[d])
+            for d in range(nz - 1)
+        ]
+
+    def finish(c):
+        whole = sv[c, z]
+        for d in range(nz - 1):
+            to_z[c][d].wait_recv()
+            whole = whole + rb3[c, d].astype(f32)
+        ost[:, pl.ds(c * cw, cw)] = whole
+
+    for c in range(CHUNKS):
+        down(c)
+        if c >= 1:
+            stage_1(c - 1)
+    stage_1(CHUNKS - 1)
+    for c in range(CHUNKS):
+        stage_2(c)
+    for c in range(CHUNKS):
+        stage_3(c)
+    for c in range(CHUNKS):
+        finish(c)
+    for s in range(steps):
+        out_ref[s] = ost[pl.ds(s * rows, rows), :].astype(bf16)
+    for copy in started:
+        copy.wait_send()
+
+
+def fused_on_device(tokens, norm_gain, expert_ids, route_weights, w_gate, w_up, w_down):
+    steps, rows, width = tokens.shape[0], tokens.shape[3], tokens.shape[4]
+    nz = lax.axis_size("ep") // 2
+    local_experts, hidden_units = w_gate.shape[0], w_gate.shape[1]
+    own_rows = steps * rows
+    cw = width // CHUNKS
+    total = 8 * nz * own_rows
+    f32, bf16 = jnp.float32, jnp.bfloat16
+    vmem = pl.BlockSpec(memory_space=pltpu.VMEM)
+    hbm = pl.BlockSpec(memory_space=pl.ANY)
+    grid_rows = (nz, own_rows, cw)
+    out = pl.pallas_call(
+        fused_kernel,
+        out_shape=jax.ShapeDtypeStruct((steps, rows, width), bf16),
+        in_specs=[vmem] * 4 + [hbm] * 3,
+        out_specs=vmem,
+        scratch_shapes=[
+            pltpu.VMEM((2 * local_experts, hidden_units, width), bf16),
+            pltpu.VMEM((local_experts * hidden_units, width), bf16),
+            pltpu.VMEM((CHUNKS, 2, 2, 2) + grid_rows, bf16),
+            pltpu.VMEM((2, 2, 2, nz, own_rows, LANES), bf16),
+            pltpu.VMEM((total, cw), bf16),
+            pltpu.VMEM((2 * local_experts, total, hidden_units), f32),
+            pltpu.VMEM((total, local_experts * hidden_units), bf16),
+            pltpu.VMEM((own_rows, width), f32),
+            pltpu.VMEM((own_rows, LANES), f32),
+            pltpu.VMEM((CHUNKS, 2, 2, 2) + grid_rows, bf16),
+            pltpu.VMEM((CHUNKS, 2, 2) + grid_rows, bf16),
+            pltpu.VMEM((CHUNKS, 2) + grid_rows, bf16),
+            pltpu.VMEM((CHUNKS, 2) + grid_rows, bf16),
+            pltpu.VMEM((CHUNKS,) + grid_rows, bf16),
+            pltpu.VMEM((CHUNKS,) + grid_rows, bf16),
+            pltpu.VMEM((CHUNKS,) + grid_rows, bf16),
+            pltpu.VMEM((CHUNKS,) + grid_rows, f32),
+            pltpu.VMEM((CHUNKS, nz - 1, own_rows, cw), bf16),
+            pltpu.VMEM((own_rows, width), f32),
+            pltpu.SemaphoreType.DMA((3 * local_experts,)),
+            pltpu.SemaphoreType.DMA((CHUNKS + 1, nz + 4)),
+            pltpu.SemaphoreType.DMA((CHUNKS + 1, nz + 4)),
+            pltpu.SemaphoreType.DMA((CHUNKS, nz + 2)),
+            pltpu.SemaphoreType.DMA((CHUNKS, nz + 2)),
+        ],
+        compiler_params=pltpu.CompilerParams(
+            collective_id=0, has_side_effects=True, vmem_limit_bytes=60 * 1024 * 1024
+        ),
+    )(
+        tokens[:, 0, 0],
+        norm_gain[None, :],
+        expert_ids[:, 0],
+        route_weights[:, 0],
+        w_gate,
+        w_up,
+        w_down,
+    )
+    return out[:, None, None]
+
+
+def on_device(tokens, norm_gain, expert_ids, route_weights, w_gate, w_up, w_down):
+    ep_size, rep_size = lax.axis_size("ep"), lax.axis_size("rep")
+    own_rows = tokens.shape[0] * tokens.shape[3]
+    experts = w_gate.shape[0] * ep_size
+    dense = (
+        rep_size == 4
+        and ep_size % 2 == 0
+        and own_rows == 8
+        and experts <= min(HALF, 4 * expert_ids.shape[4])
+        and own_rows * rep_size * ep_size <= 512
+        and tokens.shape[4] % (2 * CHUNKS * LANES) == 0
+        and w_gate.shape[1] % LANES == 0
+    )
+    run = fused_on_device if dense else routed_on_device
+    return run(tokens, norm_gain, expert_ids, route_weights, w_gate, w_up, w_down)
+
+
 def solution(mesh):
     return jax.shard_map(
         on_device,

time: 220 us -> 50.2 us (0.23)
  waiting for transfers between devices: 79.2 us -> 0 us
  Pallas kernels: 0 us -> 48.5 us
  local copies, waits for them, and re-layouts: 36.5 us -> 1.49 us
  matrix products: 32.4 us -> 0 us
  starting transfers between devices: 26.4 us -> 0 us
  blocking collectives: 21.5 us -> 0 us
  between operations: 13.7 us -> 0.01 us
  other arithmetic: 9.1 us -> 0 us
    pallas_call x0 -> x1, Pallas kernels: none -> 48.5 us  [fused_on_device(): pl.pallas_call(fused_kernel, out_shape=jax.ShapeDtypeStruct((steps, rows,...]
    reduce_scatter x2 -> x0, waiting for transfers between devices: 40.5 us -> none  [on_device(): lax.psum_scatter(results_out.astype(jnp.float32).astype(jnp.bfloat16), 'r...]
    dot_general x8 -> x0, matrix products: 32.4 us -> none  [the longest x4 20.1 us: expert_partial(): jnp.dot(hidden, down_weight, preferred_element_type=jnp.float32)]
    all_to_all x6 -> x0, starting transfers between devices: 25.8 us -> none  [the longest x2 9.22 us: on_device(): lax.all_to_all(summed.astype(jnp.bfloat16), 'ep', split_axis=0, concat_ax...]
    all_to_all x6 -> x0, waiting for transfers between devices: 24.4 us -> none  [the longest x1 11 us: on_device(): lax.all_to_all(outgoing, 'ep', split_axis=0, concat_axis=0, tiled=True)]
    all_to_all x2 -> x0, blocking collectives: 21.5 us -> none  [the longest x1 14.2 us: on_device(): lax.all_to_all(outgoing, 'ep', split_axis=0, concat_axis=0, tiled=True)]
    slice x7 -> x0, local copies, waits for them, and re-layouts: 19.5 us -> none  [the longest x2 15.2 us: on_device(): slot_rows = arrived[:, local_slot].reshape(ep_size * capacity, model_width)]
    all_gather x2 -> x0, waiting for transfers between devices: 13.6 us -> none  [on_device(): arrived = lax.all_gather(received, 'rep', axis=3, tiled=True)]
  transfers between devices with their start and end apart: 10 -> 0, of which waited for: 9 -> 0; matrix products, arithmetic and copies ran while one was open for 33% -> 0% of each run, Pallas kernels for 0% -> 0%
where the time goes in v1:
time: 50.2 us; the launch traced here: 50 us
  Pallas kernels  48.5 us (97%)
  local copies, waits for them, and re-layouts  1.49 us (3%)
    pallas_call x1, Pallas kernels, fused_on_device(): pl.pallas_call(fused_kernel, out_shape=jax.ShapeDtypeStruct((steps, rows,...  48.5 us
    unnamed x1, local copies, waits for them, and re-layouts  1.49 us

profile of v1, /device:TPU:0, one launch (start us, length us, event | category | flops | bytes accessed | tf_op | source)
XLA Modules:
  0.0 50.0 jit_solution(11083589864762643299)
XLA Ops:
  0.0 48.5 %shard_map.73 = bf16[2,4,4096]{2,1,0:T(4,128)(2,1)} custom-call(bf16[2,4,4096]{2,1,0:T(4,128)(2,1)} %bitcast.8, f32[1,4096]{1,0:T(1,128)} %bitcast.9, s32[2,4,4,8]{3,2,1,0:T(4,128)} %bitcast.10, f32[2,4,4,8]{3,2,1,0:T(4,128)} %bitcast.11, bf16[2,384,4096]{2,1,0:T(8,128)(2,1)} %gate_hbm.1, bf16[2,384,4096]{2,1,0:T(8,128)(2,1)} %up_hbm.1, ...), custom_call_target="tpu_custom_call" | custom-call | tf_op jit(solution)/shard_map/pallas_call | solution.py:341
  48.6 1.5 %copy.10 = bf16[2,1,1,4,4096]{4,3,2,1,0:T(4,128)(2,1)} copy(bf16[2,1,1,4,4096]{4,3,2,1,0:T(4,128)(2,1)} %bitcast.7) | data formatting | bytes 131072

commit v2 on v1

--- a/solution.py
+++ b/solution.py
@@ -151,9 +151,45 @@
     for load in loads + downs:
         load.start()
 
+    for s in range(steps):
+        nrm[pl.ds(s * rows, rows), :] = tok_ref[s].astype(f32)
+    values = nrm[...]
+    scaled = lax.rsqrt(jnp.mean(values * values, axis=-1, keepdims=True) + epsilon)
+    for c in range(CHUNKS):
+        cols = pl.ds(c * cw, cw)
+        xg[c, core, y, x, z] = (nrm[:, cols] * scaled * gain_ref[:, cols]).astype(bf16)
+    pl.semaphore_wait(barrier, len(everyone))
+
+    started = []
+
+    def send(src, dst, send_sem, recv_sem, device):
+        copy = pltpu.make_async_remote_copy(
+            src_ref=src, dst_ref=dst, send_sem=send_sem, recv_sem=recv_sem,
+            device_id=device, device_id_type=pl.DeviceIdType.MESH,
+        )
+        copy.start()
+        started.append(copy)
+        return copy
+
+    bufs = [xg.at[c] for c in range(CHUNKS)] + [wx]
+    order = list(range(CHUNKS)) + [CHUNKS]
+    x_first = [c % 2 == 0 for c in range(CHUNKS)] + [False]
+    first_device = [over_x if flag else over_y for flag in x_first]
+    second_device = [over_y if flag else over_x for flag in x_first]
+
+    hop_z, hop_1, hop_2, share_1, share_2, share_3 = {}, {}, {}, {}, {}, {}
+
+    def ag_send_to(c, slot, where, device):
+        ref = bufs[c].at[where]
+        return send(ref, ref, ag_send.at[c, slot], ag_recv.at[c, slot], device)
+
+    def hop_along_z(c):
+        hop_z[c] = [ag_send_to(c, d, (core, y, x, z), along_z[d]) for d in range(nz - 1)]
+
+    for c in order[:-1]:
+        hop_along_z(c)
     lane = lax.broadcasted_iota(jnp.int32, (rows, LANES), 1)
     for s in range(steps):
-        nrm[pl.ds(s * rows, rows), :] = tok_ref[s].astype(f32)
         weights_now = rw_ref[s, rep]
         ids_now = ids_ref[s, rep]
         shares = weights_now / jnp.sum(weights_now, axis=1, keepdims=True)
@@ -165,38 +201,7 @@
     high = dense.astype(bf16).astype(f32)
     wide_lane = lax.broadcasted_iota(jnp.int32, (own_rows, LANES), 1)
     wx[core, y, x, z] = jnp.where(wide_lane < HALF, high, dense - high).astype(bf16)
-    values = nrm[...]
-    scaled = lax.rsqrt(jnp.mean(values * values, axis=-1, keepdims=True) + epsilon)
-    for c in range(CHUNKS):
-        cols = pl.ds(c * cw, cw)
-        xg[c, core, y, x, z] = (nrm[:, cols] * scaled * gain_ref[:, cols]).astype(bf16)
-    pl.semaphore_wait(barrier, len(everyone))
-
-    started = []
-
-    def send(src, dst, send_sem, recv_sem, device):
-        copy = pltpu.make_async_remote_copy(
-            src_ref=src, dst_ref=dst, send_sem=send_sem, recv_sem=recv_sem,
-            device_id=device, device_id_type=pl.DeviceIdType.MESH,
-        )
-        copy.start()
-        started.append(copy)
-        return copy
-
-    bufs = [xg.at[c] for c in range(CHUNKS)] + [wx]
-    order = [CHUNKS] + list(range(CHUNKS))
-    x_first = [c % 2 == 0 for c in range(CHUNKS)] + [False]
-    first_device = [over_x if flag else over_y for flag in x_first]
-    second_device = [over_y if flag else over_x for flag in x_first]
-
-    hop_z, hop_1, hop_2, share_1, share_2, share_3 = {}, {}, {}, {}, {}, {}
-
-    def ag_send_to(c, slot, where, device):
-        ref = bufs[c].at[where]
-        return send(ref, ref, ag_send.at[c, slot], ag_recv.at[c, slot], device)
-
-    for c in order:
-        hop_z[c] = [ag_send_to(c, d, (core, y, x, z), along_z[d]) for d in range(nz - 1)]
+    hop_along_z(CHUNKS)
     for c in order:
         for copy in hop_z[c]:
             copy.wait_recv()
@@ -222,16 +227,13 @@
 
     def gate_up(c):
         arrived(c)
-        xs[...] = xg[c].astype(f32).reshape(total, cw).astype(bf16)
+        xs[...] = xg[c].astype(f32).reshape(total, cw).astype(bf16).T
         if c == 0:
             for load in loads:
                 load.wait()
 
         def one(i, carry):
-            part = lax.dot_general(
-                xs[...], wgu[i, :, pl.ds(c * cw, cw)],
-                (((1,), (1,)), ((), ())), preferred_element_type=f32,
-            )
+            part = jnp.dot(wgu[i, :, pl.ds(c * cw, cw)], xs[...], preferred_element_type=f32)
             acc[i] = part if c == 0 else acc[i] + part
             return carry
 
@@ -239,19 +241,20 @@
 
     for at, c in enumerate(order):
         finish_gather(c)
-        if at >= 2:
+        if at >= 1:
             gate_up(order[at - 1])
-    gate_up(order[-1])
     arrived(CHUNKS)
 
-    row_weights = wx[...].astype(f32).reshape(total, LANES)
-    all_lane = lax.broadcasted_iota(jnp.int32, (total, LANES), 1) & (HALF - 1)
+    row_weights = wx[...].astype(f32).reshape(total, LANES).T
+    all_lane = lax.broadcasted_iota(jnp.int32, (LANES, total), 0) & (HALF - 1)
     for j in range(local_experts):
         mine = jnp.sum(
-            jnp.where(all_lane == ep * local_experts + j, row_weights, 0.0), axis=1, keepdims=True
+            jnp.where(all_lane == ep * local_experts + j, row_weights, 0.0), axis=0, keepdims=True
         )
         gate_out, up_out = acc[j], acc[local_experts + j]
-        hs[:, pl.ds(j * hidden_units, hidden_units)] = (jax.nn.silu(gate_out) * up_out * mine).astype(bf16)
+        hs[:, pl.ds(j * hidden_units, hidden_units)] = (
+            jax.nn.silu(gate_out) * up_out * mine
+        ).T.astype(bf16)
     for load in downs:
         load.wait()
 
@@ -322,7 +325,7 @@
     for c in range(CHUNKS):
         finish(c)
     for s in range(steps):
-        out_ref[s] = ost[pl.ds(s * rows, rows), :].astype(bf16)
+        out_ref[s] = ost[pl.ds(s * rows, rows), :]
     for copy in started:
         copy.wait_send()
 
@@ -340,7 +343,7 @@
     grid_rows = (nz, own_rows, cw)
     out = pl.pallas_call(
         fused_kernel,
-        out_shape=jax.ShapeDtypeStruct((steps, rows, width), bf16),
+        out_shape=jax.ShapeDtypeStruct((steps, rows, width), f32),
         in_specs=[vmem] * 4 + [hbm] * 3,
         out_specs=vmem,
         scratch_shapes=[
@@ -348,8 +351,8 @@
             pltpu.VMEM((local_experts * hidden_units, width), bf16),
             pltpu.VMEM((CHUNKS, 2, 2, 2) + grid_rows, bf16),
             pltpu.VMEM((2, 2, 2, nz, own_rows, LANES), bf16),
-            pltpu.VMEM((total, cw), bf16),
-            pltpu.VMEM((2 * local_experts, total, hidden_units), f32),
+            pltpu.VMEM((cw, total), bf16),
+            pltpu.VMEM((2 * local_experts, hidden_units, total), f32),
             pltpu.VMEM((total, local_experts * hidden_units), bf16),
             pltpu.VMEM((own_rows, width), f32),
             pltpu.VMEM((own_rows, LANES), f32),
@@ -381,7 +384,7 @@
         w_up,
         w_down,
     )
-    return out[:, None, None]
+    return out.astype(bf16)[:, None, None]
 
 
 def on_device(tokens, norm_gain, expert_ids, route_weights, w_gate, w_up, w_down):

time: 50.2 us -> 49.7 us (0.990)
  other arithmetic: 0 us -> 1.56 us
  local copies, waits for them, and re-layouts: 1.49 us -> 0 us
  Pallas kernels: 48.5 us -> 47.9 us
    broadcast_in_dim x0 -> x1, other arithmetic: none -> 1.56 us  [fused_on_device(): return out.astype(bf16)[:, None, None]]
    unnamed x1 -> x0, local copies, waits for them, and re-layouts: 1.49 us -> none
    pallas_call x1, Pallas kernels: 48.5 us -> 47.9 us  [fused_on_device(): pl.pallas_call(fused_kernel, out_shape=jax.ShapeDtypeStruct((steps, rows,...]
where the time goes in v2:
time: 49.7 us; the launch traced here: 49.5 us
  Pallas kernels  47.9 us (96%)
  other arithmetic  1.56 us (3%)
    pallas_call x1, Pallas kernels, fused_on_device(): pl.pallas_call(fused_kernel, out_shape=jax.ShapeDtypeStruct((steps, rows,...  47.9 us
    broadcast_in_dim x1, other arithmetic, fused_on_device(): return out.astype(bf16)[:, None, None]  1.56 us

profile of v2, /device:TPU:0, one launch (start us, length us, event | category | flops | bytes accessed | tf_op | source)
XLA Modules:
  0.0 49.5 jit_solution(6767065441411426716)
XLA Ops:
  0.0 47.9 %shard_map.73 = f32[2,4,4096]{2,1,0:T(4,128)} custom-call(bf16[2,4,4096]{2,1,0:T(4,128)(2,1)} %bitcast.8, f32[1,4096]{1,0:T(1,128)} %bitcast.9, s32[2,4,4,8]{3,2,1,0:T(4,128)} %bitcast.10, f32[2,4,4,8]{3,2,1,0:T(4,128)} %bitcast.11, bf16[2,384,4096]{2,1,0:T(8,128)(2,1)} %gate_hbm.1, bf16[2,384,4096]{2,1,0:T(8,128)(2,1)} %up_hbm.1, bf16[2,384,4096]{2,1,0:T(8,128)(2,1)} %down_hbm.1), custom_call_target="tpu_custom_call" | custom-call | tf_op jit(solution)/shard_map/pallas_call | solution.py:344
  47.9 1.6 %convert_bitcast_fusion = bf16[2,1,1,4,4096]{4,3,2,1,0:T(4,128)(2,1)} fusion(f32[2,4,4096]{2,1,0:T(4,128)} %shard_map.73), kind=kLoop, calls=%fused_computation | loop fusion | flops 32768 | bytes 196608 | tf_op jit(solution)/shard_map/broadcast_in_dim | solution.py:387

commit v3 on v2

--- a/solution.py
+++ b/solution.py
@@ -173,7 +173,7 @@
 
     bufs = [xg.at[c] for c in range(CHUNKS)] + [wx]
     order = list(range(CHUNKS)) + [CHUNKS]
-    x_first = [c % 2 == 0 for c in range(CHUNKS)] + [False]
+    x_first = [(c + 1) % 4 < 2 for c in range(CHUNKS)] + [False]
     first_device = [over_x if flag else over_y for flag in x_first]
     second_device = [over_y if flag else over_x for flag in x_first]
 
@@ -185,6 +185,7 @@
 
     def hop_along_z(c):
         hop_z[c] = [ag_send_to(c, d, (core, y, x, z), along_z[d]) for d in range(nz - 1)]
+        hop_1[c] = [ag_send_to(c, nz - 1, (core, y, x, z), first_device[c])]
 
     for c in order[:-1]:
         hop_along_z(c)
@@ -203,23 +204,25 @@
     wx[core, y, x, z] = jnp.where(wide_lane < HALF, high, dense - high).astype(bf16)
     hop_along_z(CHUNKS)
     for c in order:
-        for copy in hop_z[c]:
+        for d, copy in enumerate(hop_z[c]):
             copy.wait_recv()
-        hop_1[c] = ag_send_to(c, nz - 1, (core, y, x), first_device[c])
-        share_1[c] = ag_send_to(c, nz + 1, (core, y, x), partner)
+            came_from = (core, y, x, (z - d - 1 + nz) % nz)
+            hop_1[c].append(ag_send_to(c, nz + d, came_from, first_device[c]))
+        share_1[c] = ag_send_to(c, 2 * nz, (core, y, x), partner)
     for c in order:
-        hop_1[c].wait_recv()
+        for copy in hop_1[c]:
+            copy.wait_recv()
         if x_first[c]:
-            hop_2[c] = ag_send_to(c, nz, (core, y), second_device[c])
-            share_2[c] = ag_send_to(c, nz + 2, (core, y, 1 - x), partner)
+            hop_2[c] = ag_send_to(c, 2 * nz - 1, (core, y), second_device[c])
+            share_2[c] = ag_send_to(c, 2 * nz + 1, (core, y, 1 - x), partner)
         else:
-            hop_2[c] = ag_send_to(c, nz, (core, slice(None), x), second_device[c])
-            share_2[c] = ag_send_to(c, nz + 2, (core, 1 - y, x), partner)
+            hop_2[c] = ag_send_to(c, 2 * nz - 1, (core, slice(None), x), second_device[c])
+            share_2[c] = ag_send_to(c, 2 * nz + 1, (core, 1 - y, x), partner)
 
     def finish_gather(c):
         hop_2[c].wait_recv()
         where = (core, 1 - y) if x_first[c] else (core, slice(None), 1 - x)
-        share_3[c] = ag_send_to(c, nz + 3, where, partner)
+        share_3[c] = ag_send_to(c, 2 * nz + 2, where, partner)
 
     def arrived(c):
         for copy in (share_1[c], share_2[c], share_3[c]):
@@ -367,8 +370,8 @@
             pltpu.VMEM((CHUNKS, nz - 1, own_rows, cw), bf16),
             pltpu.VMEM((own_rows, width), f32),
             pltpu.SemaphoreType.DMA((3 * local_experts,)),
-            pltpu.SemaphoreType.DMA((CHUNKS + 1, nz + 4)),
-            pltpu.SemaphoreType.DMA((CHUNKS + 1, nz + 4)),
+            pltpu.SemaphoreType.DMA((CHUNKS + 1, 2 * nz + 3)),
+            pltpu.SemaphoreType.DMA((CHUNKS + 1, 2 * nz + 3)),
             pltpu.SemaphoreType.DMA((CHUNKS, nz + 2)),
             pltpu.SemaphoreType.DMA((CHUNKS, nz + 2)),
         ],

time: 49.7 us -> 49.1 us (0.988)
  Pallas kernels: 47.9 us -> 47.3 us
    pallas_call x1, Pallas kernels: 47.9 us -> 47.3 us  [fused_on_device(): pl.pallas_call(fused_kernel, out_shape=jax.ShapeDtypeStruct((steps, rows,...]
where the time goes in v3:
time: 49.1 us; the launch traced here: 48.9 us
  Pallas kernels  47.3 us (96%)
  other arithmetic  1.56 us (3%)
    pallas_call x1, Pallas kernels, fused_on_device(): pl.pallas_call(fused_kernel, out_shape=jax.ShapeDtypeStruct((steps, rows,...  47.3 us
    broadcast_in_dim x1, other arithmetic, fused_on_device(): return out.astype(bf16)[:, None, None]  1.56 us

profile of v3, /device:TPU:0, one launch (start us, length us, event | category | flops | bytes accessed | tf_op | source)
XLA Modules:
  0.0 48.9 jit_solution(13449821720550022324)
XLA Ops:
  0.0 47.3 %shard_map.73 = f32[2,4,4096]{2,1,0:T(4,128)} custom-call(bf16[2,4,4096]{2,1,0:T(4,128)(2,1)} %bitcast.8, f32[1,4096]{1,0:T(1,128)} %bitcast.9, s32[2,4,4,8]{3,2,1,0:T(4,128)} %bitcast.10, f32[2,4,4,8]{3,2,1,0:T(4,128)} %bitcast.11, bf16[2,384,4096]{2,1,0:T(8,128)(2,1)} %gate_hbm.1, bf16[2,384,4096]{2,1,0:T(8,128)(2,1)} %up_hbm.1, bf16[2,384,4096]{2,1,0:T(8,128)(2,1)} %down_hbm.1), custom_call_target="tpu_custom_call" | custom-call | tf_op jit(solution)/shard_map/pallas_call | solution.py:347
  47.3 1.6 %convert_bitcast_fusion = bf16[2,1,1,4,4096]{4,3,2,1,0:T(4,128)(2,1)} fusion(f32[2,4,4096]{2,1,0:T(4,128)} %shard_map.73), kind=kLoop, calls=%fused_computation | loop fusion | flops 32768 | bytes 196608 | tf_op jit(solution)/shard_map/broadcast_in_dim | solution.py:390
